TPU v7x, 256 devices: a whole 4x4x8 slice. The times are simulated.
256 devices in a mesh: fsdp: 16 (over y, z_lo, core), uly: 4 (over x), blk: 4 (over z_hi).
Axes of the slice: x: 4, y: 4, z: 8 (z_hi: 4, z_lo: 2; z = z_hi * 2 + z_lo), core: 2. Of those that a mesh axis runs over, the one named last changes fastest.
Arguments:
- latents: bfloat16 [16, 3072, 3072], P('fsdp', ('uly', 'blk')), may hold values from -40 to 40
- sampler_noise: bfloat16 [16, 3072, 3072], P('fsdp', ('uly', 'blk')), may hold values from -6 to 6
- query_key_value_weight: bfloat16 [3, 3072, 1536], P(None, 'fsdp', 'uly'), may hold values from -0.375 to 0.375
- output_weight: bfloat16 [3072, 1536], P('fsdp', 'uly'), may hold values from -0.15625 to 0.15625
- adapter_down_map: bfloat16 [64, 1536], P(None, 'uly'), may hold values from -0.15625 to 0.15625
- adapter_up_map: bfloat16 [64, 3072], replicated, may hold values from -0.75 to 0.75
- valid_token_count: int32 [16], P('fsdp'), may hold values from 1536 to 3072
- advantage: float32 [16], P('fsdp'), may hold values from -3 to 3
- timestep_index: int32 [1], replicated, may hold values from 1 to 15
Outputs:
- next_latents: bfloat16 [16, 3072, 3072], P('fsdp', ('uly', 'blk'))
- log_ratio: float32 [16], P('fsdp')
- grad_down: float32 [64, 1536], P(None, 'uly')
- grad_up: float32 [64, 3072], replicated
All inputs are finite; a program needn't handle non-finite values.
Results may differ from a plain program's by a relative error of at most 0.0055.
The roundings to bfloat16 on the way count: a program that leaves them out, or rounds other values in their place, can miss the bound.
Values may be sent and summed in bfloat16 or wider, within the bound.
No kernel may reach another device: no remote copies, remote signals or barrier semaphores. Data moves between devices by JAX's collectives and lax.ppermute only.
A program may use at most 128 MiB of HBM per device.

v0:
```python
import math
import jax
import jax.numpy as jnp
from jax import lax
from jax.sharding import PartitionSpec as P

HEAD_SIZE = 128
STEPS = 16
noise_level = 0.7
loss_scale = 4194304.0
rms_eps = 1e-06


def shards(
    latents,
    sampler_noise,
    query_key_value_weight,
    output_weight,
    adapter_down_map,
    adapter_up_map,
    valid_token_count,
    advantage,
    timestep_index,
):
    current = latents[0].astype(jnp.float32)
    rows = current.shape[0]
    width = current.shape[1]
    normed = (current * lax.rsqrt(jnp.mean(current * current, -1, keepdims=True) + rms_eps)).astype(
        jnp.bfloat16
    )
    gathered = lax.all_gather(normed, "uly", axis=0, tiled=True)
    projected = jnp.einsum(
        "td,kdh->kth",
        gathered,
        lax.all_gather(query_key_value_weight, "fsdp", axis=1, tiled=True),
        preferred_element_type=jnp.float32,
    ).astype(jnp.bfloat16)
    query_rows = projected[0]
    key_rows, value_rows = (
        lax.all_gather(projected[1], "blk", axis=0, tiled=True),
        lax.all_gather(projected[2], "blk", axis=0, tiled=True),
    )
    uly_count = lax.axis_size("uly")
    blk_count = lax.axis_size("blk")
    uly_id = lax.axis_index("uly")
    blk_id = lax.axis_index("blk")
    limit = valid_token_count[0]
    group_rows = uly_count * rows
    key_index = jnp.arange(key_rows.shape[0], dtype=jnp.int32)
    key_pos = (
        key_index % group_rows // rows * blk_count + key_index // group_rows
    ) * rows + key_index % rows
    key_ok = (key_pos < limit)[None, None, :]
    heads_here = query_rows.shape[1] // HEAD_SIZE
    query_split = query_rows.reshape(query_rows.shape[0], heads_here, HEAD_SIZE)
    key_split = key_rows.reshape(key_rows.shape[0], heads_here, HEAD_SIZE)
    value_split = value_rows.reshape(value_rows.shape[0], heads_here, HEAD_SIZE)
    scores = jnp.einsum(
        "qhd,khd->hqk", query_split, key_split, preferred_element_type=jnp.float32
    ) * (1.0 / math.sqrt(HEAD_SIZE))
    masked = jnp.where(key_ok, scores, -1e30)
    row_max = jnp.max(masked, -1, keepdims=True)
    exp_terms = jnp.where(key_ok, jnp.exp(masked - row_max), 0.0)
    weights = (exp_terms / jnp.sum(exp_terms, -1, keepdims=True)).astype(jnp.bfloat16)
    attention_output = jnp.einsum(
        "hqk,khd->qhd", weights, value_split, preferred_element_type=jnp.float32
    )
    attention_output = attention_output.astype(jnp.bfloat16).reshape(
        query_rows.shape[0], heads_here * HEAD_SIZE
    )
    weight_cols = lax.all_gather(output_weight, "fsdp", axis=0, tiled=True)
    contract_product = (((1,), (1,)), ((), ()))
    own_heads = lax.all_to_all(attention_output, "uly", split_axis=0, concat_axis=1, tiled=True)
    weight_full, down_full = (
        lax.all_gather(weight_cols, "uly", axis=1, tiled=True),
        lax.all_gather(adapter_down_map, "uly", axis=1, tiled=True),
    )
    velocity = lax.dot_general(
        own_heads, weight_full, contract_product, preferred_element_type=jnp.float32
    )
    narrow_projection = lax.dot_general(
        own_heads, down_full, contract_product, preferred_element_type=jnp.float32
    ).astype(jnp.bfloat16)
    adapter_result = jnp.dot(narrow_projection, adapter_up_map, preferred_element_type=jnp.float32)
    step_float = timestep_index[0].astype(jnp.float32)
    time_now = 1.0 - step_float / STEPS
    step_size = 1.0 / STEPS
    noise_std = noise_level * jnp.sqrt(time_now / (1.0 - time_now))
    drift_gain = 1.0 + noise_level**2 / 2.0
    ratio_gain = jnp.sqrt(step_size) * drift_gain / noise_std
    noise_f = sampler_noise[0].astype(jnp.float32)
    moved = current - step_size * (
        drift_gain * velocity + noise_level**2 * current / (2.0 * (1.0 - time_now))
    )
    next_latents = (moved + noise_std * jnp.sqrt(step_size) * noise_f).astype(jnp.bfloat16)[None]
    standard = noise_f + ratio_gain * adapter_result
    tok_pos = (uly_id * blk_count + blk_id) * rows + jnp.arange(rows, dtype=jnp.int32)
    tok_ok = (tok_pos < limit)[:, None]
    valid_len = limit.astype(jnp.float32)
    partial_log = jnp.sum(jnp.where(tok_ok, noise_f * noise_f - standard * standard, 0.0)) / (
        2.0 * valid_len * width
    )
    log_ratio = lax.psum(partial_log, ("uly", "blk"))
    coef = (
        loss_scale
        * advantage[0]
        * jnp.exp(log_ratio)
        * ratio_gain
        / (lax.axis_size("fsdp") * valid_len * width)
    )
    delta_gradient = (jnp.where(tok_ok, standard, 0.0) * coef).astype(jnp.bfloat16)
    first_axis = (((0,), (0,)), ((), ()))
    up_part = lax.dot_general(
        narrow_projection, delta_gradient, first_axis, preferred_element_type=jnp.float32
    )
    narrow_gradient = lax.dot_general(
        delta_gradient, adapter_up_map, contract_product, preferred_element_type=jnp.float32
    ).astype(jnp.bfloat16)
    down_part = lax.dot_general(
        narrow_gradient, own_heads, first_axis, preferred_element_type=jnp.float32
    )
    grad_up, down_total = lax.psum((up_part, down_part), ("fsdp", "uly", "blk"))
    local_columns = adapter_down_map.shape[1]
    grad_down = lax.dynamic_slice_in_dim(down_total, uly_id * local_columns, local_columns, 1)
    return (next_latents, jnp.reshape(log_ratio, (1,)), grad_down, grad_up)


def solution(mesh):
    placed = (
        P("fsdp", ("uly", "blk"), None),
        P("fsdp", ("uly", "blk"), None),
        P(None, "fsdp", "uly"),
        P("fsdp", "uly"),
        P(None, "uly"),
        P(),
        P("fsdp"),
        P("fsdp"),
        P(),
    )
    return jax.shard_map(
        shards,
        mesh=mesh,
        in_specs=placed,
        out_specs=(P("fsdp", ("uly", "blk"), None), P("fsdp"), P(None, "uly"), P()),
        check_vma=False,
    )
```

profile of v0, /device:TPU:1, one launch (start us, length us, event | category | flops | bytes accessed | tf_op | source)
XLA Modules:
  0.0 696.5 jit_solution(7782017306988435983)
XLA Ops:
  7.2 1.6 fusion.19
  8.9 2.6 fusion.20
  11.5 0.7 all-gather.11.cloned.1.call-update
  12.3 58.1 %all-gather.9.cloned.1.call-done = bf16[768,3072]{1,0:T(8,128)(2,1)} async-done(((bf16[192,3072]{1,0:T(8,128)(2,1)}), bf16[768,3072]{1,0:T(8,128)(2,1)}) %all-gather.9.cloned.1.call-update) | async-done | bytes 4718608 | tf_op jit(solution)/shard_map/all_gather | solution.py:31
  70.3 51.3 %all-gather.11.cloned.1.call-done = bf16[3,3072,384]{2,1,0:T(8,128)(2,1)} async-done(((bf16[3,192,384]{2,1,0:T(8,128)(2,1)}), bf16[3,3072,384]{2,1,0:T(8,128)(2,1)}) %all-gather.11.cloned.1.call-update) | async-done | bytes 7077904 | tf_op jit(solution)/shard_map/all_gather | solution.py:35
  121.7 10.3 %convert_bitcast_fusion = bf16[3,768,384]{1,2,0:T(8,128)(2,1)S(1)} fusion(bf16[3,3072,384]{2,1,0:T(8,128)(2,1)} %all-gather.11.cloned.1.call-done, bf16[768,3072]{1,0:T(8,128)(2,1)} %all-gather.9.cloned.1.call-done), kind=kOutput, calls=%fused_computation.33 | convolution fusion | flops 5436702720 | bytes 13565952 | tf_op jit(solution)/shard_map/td,kdh->kth/dot_general | solution.py:32
  132.0 1.1 fusion.53
  133.2 0.5 all-gather.17.cloned.1.call-update
  133.7 0.2 all-gather.13.cloned.1.call-start
  133.9 0.4 all-gather.13.cloned.1.call-update
  135.0 50.7 %all-gather.19.cloned.1.call-done = bf16[1,3072,384]{1,2,0:T(8,128)(2,1)} async-done(((bf16[1,768,384]{1,2,0:T(8,128)(2,1)}), bf16[1,3072,384]{1,2,0:T(8,128)(2,1)}) %all-gather.19.cloned.1.call-update) | async-done | bytes 2359312 | tf_op jit(solution)/shard_map/all_gather | solution.py:40
  185.6 16.2 %fusion.54 = (f32[3,768]{1,0:T(4,128)S(1)}, f32[3,768,3072]{2,1,0:T(8,128)}) fusion(pred[3072]{0:T(1024)(128)(4,1)S(1)} %fusion.47, bf16[768,3,128]{0,2,1:T(8,128)(2,1)S(1)} %bitcast.55, bf16[3072,3,128]{0,2,1:T(8,128)(2,1)} %bitcast.56), kind=kOutput, calls=%fused_computation.75 | convolution fusion | flops 1847331840 | bytes 31272960 | tf_op jit(solution)/shard_map/sub | solution.py:63
  201.9 44.3 %all-gather.17.cloned.1.call-done = bf16[1,3072,384]{1,2,0:T(8,128)(2,1)} async-done(((bf16[1,768,384]{1,2,0:T(8,128)(2,1)}), bf16[1,3072,384]{1,2,0:T(8,128)(2,1)}) %all-gather.17.cloned.1.call-update) | async-done | bytes 2359312 | tf_op jit(solution)/shard_map/all_gather | solution.py:41
  246.2 12.1 %fusion.25 = bf16[768,3,128]{0,2,1:T(8,128)(2,1)S(1)} fusion(bf16[3072,3,128]{0,2,1:T(8,128)(2,1)} %bitcast.57, f32[3,768,3072]{2,1,0:T(8,128)} %get-tuple-element.10, f32[3,768]{1,0:T(4,128)S(1)} %get-tuple-element.9), kind=kOutput, calls=%fused_computation.35 | convolution fusion | flops 1826390016 | bytes 31269888 | tf_op jit(solution)/shard_map/hqk,khd->qhd/dot_general | solution.py:65
  258.2 0.7 reshape.95
  258.9 1.4 copy.21
  260.3 3.5 all-to-all-start
  263.8 0.0 all-reduce.3.cloned.1.call-start
  265.3 12.0 %all_gather.27 = bf16[64,1536]{1,0:T(8,128)(2,1)S(1)} all-gather(bf16[64,384]{1,0:T(8,128)(2,1)S(1)} %copy-done.3), channel_id=1, replica_groups=mesh['fsdp'=16,'uly'=4,'blk'=4] {'uly'}, dimensions={1}, use_global_device_ids=true | all-gather | bytes 245760 | tf_op jit(solution)/shard_map/all_gather | solution.py:76
  277.4 0.1 copy.22
  277.5 0.3 convolution_convert_fusion.1
  277.8 2.8 fusion.18
  281.2 36.3 %psum.21 = f32[]{:T(128)} all-reduce(f32[]{:T(128)S(6)} %div.64), channel_id=1, replica_groups=mesh['fsdp'=16,'uly'=4,'blk'=4] {'uly','blk'}, use_global_device_ids=true, to_apply=%region_4.5 | all-reduce | flops 1 | bytes 8 | tf_op jit(solution)/shard_map/psum | solution.py:103
  318.3 1.3 fusion.52
  319.6 1.7 fusion.26
  321.3 0.0 all-gather.15.cloned.1.call-start
  321.4 0.7 all-gather.15.cloned.1.call-update
  322.1 262.3 %all-reduce.3.cloned.1.call-done = (f32[64,1536]{1,0:T(8,128)}, f32[64,3072]{1,0:T(8,128)}) async-done(((f32[64,1536]{1,0:T(8,128)}, f32[64,3072]{1,0:T(8,128)}), (f32[64,1536]{1,0:T(8,128)}, f32[64,3072]{1,0:T(8,128)})) %all-reduce.3.cloned.1.call-update) | async-done | bytes 1179664 | tf_op jit(solution)/shard_map/psum | solution.py:122
  584.4 1.5 constant_dynamic-slice_fusion
  586.0 94.5 %all-gather.15.cloned.1.call-done = bf16[3072,1536]{1,0:T(8,128)(2,1)} async-done(((bf16[3072,384]{1,0:T(8,128)(2,1)}), bf16[3072,1536]{1,0:T(8,128)(2,1)}) %all-gather.15.cloned.1.call-update) | async-done | bytes 9437200 | tf_op jit(solution)/shard_map/all_gather | solution.py:75
  680.5 8.3 %fusion.13 = bf16[1,192,3072]{2,1,0:T(8,128)(2,1)} fusion(bf16[192,1536]{1,0:T(8,128)(2,1)S(1)} %bitcast.53, bf16[3072,1536]{1,0:T(8,128)(2,1)} %all-gather.15.cloned.1.call-done, bf16[1,192,3072]{2,1,0:T(8,128)(2,1)} %param.10, bf16[1,192,3072]{2,1,0:T(8,128)(2,1)S(1)} %copy-done.1, f32[]{:T(128)S(6)} %mul.121, f32[]{:T(128)S(6)} %mul.118), kind=kOutput, calls=%fused_computation.22 | convolution fusion | flops 1818427392 | bytes 13565960 | tf_op jit(solution)/shard_map/dot_general | solution.py:78
  688.8 0.9 copy.28
  (20 shorter events, 0.3 us)
Async XLA Ops:
  7.2 270.6 %copy-start = (bf16[64,3072]{1,0:T(8,128)(2,1)S(1)}, bf16[64,3072]{1,0:T(8,128)(2,1)}, u32[]{:S(2)}) copy-start(bf16[64,3072]{1,0:T(8,128)(2,1)} %param.14) | copy-start | bytes 1179652
  7.2 63.2 %all-gather.9.cloned.1.call-start = ((), (), s32[]{:S(2)}) async-start(), calls=%async_computation.1 | async-start | bytes 5898240 | tf_op jit(solution)/shard_map/all_gather | solution.py:31
  11.5 110.2 %all-gather.11.cloned.1.call-start = ((), (), s32[]{:S(2)}) async-start(), calls=%async_computation.2 | async-start | bytes 7520256 | tf_op jit(solution)/shard_map/all_gather | solution.py:35
  12.2 173.4 %all-gather.19.cloned.1.call-start = ((), (), s32[]{:S(2)}) async-start(), calls=%async_computation.6 | async-start | bytes 2949120 | tf_op jit(solution)/shard_map/all_gather | solution.py:40
  133.1 113.0 %all-gather.17.cloned.1.call-start = ((), (), s32[]{:S(2)}) async-start(), calls=%async_computation.5 | async-start | bytes 2949120 | tf_op jit(solution)/shard_map/all_gather | solution.py:41
  133.7 187.7 %all-gather.13.cloned.1.call-start = ((), (), s32[]{:S(2)}) async-start(), calls=%async_computation.3 | async-start | bytes 2506752 | tf_op jit(solution)/shard_map/all_gather | solution.py:71
  258.2 7.1 %copy-start.3 = (bf16[64,384]{1,0:T(8,128)(2,1)S(1)}, bf16[64,384]{1,0:T(8,128)(2,1)}, u32[]{:S(2)}) copy-start(bf16[64,384]{1,0:T(8,128)(2,1)} %param.13) | copy-start | bytes 147460
  260.3 17.0 %all-to-all-start = ((bf16[4,192,384]{2,1,0:T(8,128)(2,1)}), bf16[4,192,384]{2,1,0:T(8,128)(2,1)S(1)}, u32[]{:S(2)}, u32[]{:S(2)}) async-start(bf16[4,192,384]{2,1,0:T(8,128)(2,1)} %copy.21), calls=%async_computation | async-start | bytes 1179648 | tf_op jit(solution)/shard_map/all_to_all | solution.py:73
  263.8 320.6 %all-reduce.3.cloned.1.call-start = ((), (), s32[]{:S(2)}) async-start(), calls=%async_computation.7 | async-start | bytes 2359296 | tf_op jit(solution)/shard_map/psum | solution.py:122
  321.3 359.2 %copy-start.1 = (bf16[1,192,3072]{2,1,0:T(8,128)(2,1)S(1)}, bf16[1,192,3072]{2,1,0:T(8,128)(2,1)}, u32[]{:S(2)}) copy-start(bf16[1,192,3072]{2,1,0:T(8,128)(2,1)} %param.9) | copy-start | bytes 3538948
  321.3 359.2 %all-gather.15.cloned.1.call-start = ((), (), s32[]{:S(2)}) async-start(), calls=%async_computation.4 | async-start | bytes 11796480 | tf_op jit(solution)/shard_map/all_gather | solution.py:75
  586.0 102.8 %copy-start.2 = (f32[64,3072]{1,0:T(8,128)S(1)}, f32[64,3072]{1,0:T(8,128)}, u32[]{:S(2)}) copy-start(f32[64,3072]{1,0:T(8,128)} %get-tuple-element.16) | copy-start | bytes 2359300
Sparse Core Ops, SparseCore 0:
  11.6 58.6 all-gather.8
  72.1 49.4 all-gather.10
  133.3 52.3 all-gather.18
  187.9 58.2 all-gather.16
  247.8 35.5 all-gather.12
  321.4 262.9 all-reduce.2
  586.3 94.2 all-gather.14
where the time goes:
time: 697 us
  waiting for transfers between devices  564 us (81%)
  matrix products  53 us (8%)
  blocking collectives  48.4 us (7%)
  between operations  17.7 us (3%)
    psum x1, waiting for transfers between devices, shards(): grad_up, down_total = lax.psum((up_part, down_part), ('fsdp', 'uly', 'blk'))  262 us
    all_gather x1, waiting for transfers between devices, shards(): lax.all_gather(weight_cols, 'uly', axis=1, tiled=True)  94.5 us
    all_gather x1, waiting for transfers between devices, shards(): gathered = lax.all_gather(normed, 'uly', axis=0, tiled=True)  58.1 us
    all_gather x1, waiting for transfers between devices, shards(): lax.all_gather(query_key_value_weight, 'fsdp', axis=1, tiled=True)  51.3 us
    all_gather x1, waiting for transfers between devices, shards(): lax.all_gather(projected[1], 'blk', axis=0, tiled=True)  50.7 us
    all_gather x1, waiting for transfers between devices, shards(): lax.all_gather(projected[2], 'blk', axis=0, tiled=True)  44.3 us
    psum x1, blocking collectives, shards(): log_ratio = lax.psum(partial_log, ('uly', 'blk'))  36.3 us
    sub x1, matrix products, shards(): exp_terms = jnp.where(key_ok, jnp.exp(masked - row_max), 0.0)  16.2 us
  transfers between devices with their start and end apart: 8, of which 6 were waited for; matrix products, arithmetic and copies ran while one was open for 5% of the time, Pallas kernels for 0%

commit v1 on v0

--- a/solution.py
+++ b/solution.py
@@ -72,7 +72,9 @@
     contract_product = (((1,), (1,)), ((), ()))
     own_heads = lax.all_to_all(attention_output, "uly", split_axis=0, concat_axis=1, tiled=True)
     weight_full, down_full = (
-        lax.all_gather(weight_cols, "uly", axis=1, tiled=True),
+        jnp.concatenate(
+            lax.all_to_all(jnp.stack([weight_cols] * lax.axis_size("uly")), "uly", 0, 0), axis=1
+        ),
         lax.all_gather(adapter_down_map, "uly", axis=1, tiled=True),
     )
     velocity = lax.dot_general(

time: 697 us -> 724 us (1.039)
  blocking collectives: 48.4 us -> 146 us
  waiting for transfers between devices: 564 us -> 478 us
  local copies, waits for them, and re-layouts: 5.72 us -> 13.2 us
    all_gather x1, blocking collectives: 12 us -> 107 us  [shards(): lax.all_gather(adapter_down_map, 'uly', axis=1, tiled=True)]
    all_gather x1 -> x0, waiting for transfers between devices: 94.5 us -> none  [shards(): lax.all_gather(weight_cols, 'uly', axis=1, tiled=True)]
    all_gather x1, waiting for transfers between devices: 0.02 us -> 19.6 us  [shards(): weight_cols = lax.all_gather(output_weight, 'fsdp', axis=0, tiled=True)]
    psum x1, waiting for transfers between devices: 262 us -> 252 us  [shards(): grad_up, down_total = lax.psum((up_part, down_part), ('fsdp', 'uly', 'blk'))]
  transfers between devices with their start and end apart: 8 -> 8, of which waited for: 6 -> 6; matrix products, arithmetic and copies ran while one was open for 5% -> 6% of each run, Pallas kernels for 0% -> 0%
where the time goes in v1:
time: 724 us; the launch traced here: 722 us
  waiting for transfers between devices  478 us (66%)
  blocking collectives  146 us (20%)
  matrix products  53.5 us (7%)
  between operations  17.7 us (2%)
  local copies, waits for them, and re-layouts  13.2 us (2%)
  starting transfers between devices  9.84 us (1%)
    psum x1, waiting for transfers between devices, shards(): grad_up, down_total = lax.psum((up_part, down_part), ('fsdp', 'uly', 'blk'))  252 us
    all_gather x1, blocking collectives, shards(): lax.all_gather(adapter_down_map, 'uly', axis=1, tiled=True)  107 us
    all_gather x1, waiting for transfers between devices, shards(): gathered = lax.all_gather(normed, 'uly', axis=0, tiled=True)  58.1 us
    all_gather x1, waiting for transfers between devices, shards(): lax.all_gather(query_key_value_weight, 'fsdp', axis=1, tiled=True)  51.3 us
    all_gather x1, waiting for transfers between devices, shards(): lax.all_gather(projected[1], 'blk', axis=0, tiled=True)  50.7 us
    all_gather x1, waiting for transfers between devices, shards(): lax.all_gather(projected[2], 'blk', axis=0, tiled=True)  44.3 us
    psum x1, blocking collectives, shards(): log_ratio = lax.psum(partial_log, ('uly', 'blk'))  38.5 us
    all_gather x1, waiting for transfers between devices, shards(): weight_cols = lax.all_gather(output_weight, 'fsdp', axis=0, tiled=True)  19.6 us
  transfers between devices with their start and end apart: 8, of which 6 were waited for; matrix products, arithmetic and copies ran while one was open for 6% of the time, Pallas kernels for 0%

profile of v1, /device:TPU:1, one launch (start us, length us, event | category | flops | bytes accessed | tf_op | source)
XLA Modules:
  0.0 721.8 jit_solution(12990748892763849995)
XLA Ops:
  7.2 1.6 fusion.39
  8.9 2.6 fusion.40
  11.5 0.7 all-gather.10.cloned.1.call-update
  12.3 58.1 %all-gather.8.cloned.1.call-done = bf16[768,3072]{1,0:T(8,128)(2,1)} async-done(((bf16[192,3072]{1,0:T(8,128)(2,1)}), bf16[768,3072]{1,0:T(8,128)(2,1)}) %all-gather.8.cloned.1.call-update) | async-done | bytes 4718608 | tf_op jit(solution)/shard_map/all_gather | solution.py:31
  70.3 51.3 %all-gather.10.cloned.1.call-done = bf16[3,3072,384]{2,1,0:T(8,128)(2,1)} async-done(((bf16[3,192,384]{2,1,0:T(8,128)(2,1)}), bf16[3,3072,384]{2,1,0:T(8,128)(2,1)}) %all-gather.10.cloned.1.call-update) | async-done | bytes 7077904 | tf_op jit(solution)/shard_map/all_gather | solution.py:35
  121.7 10.3 %convert_bitcast_fusion = bf16[3,768,384]{1,2,0:T(8,128)(2,1)S(1)} fusion(bf16[3,3072,384]{2,1,0:T(8,128)(2,1)} %all-gather.10.cloned.1.call-done, bf16[768,3072]{1,0:T(8,128)(2,1)} %all-gather.8.cloned.1.call-done), kind=kOutput, calls=%fused_computation.36 | convolution fusion | flops 5436702720 | bytes 13565952 | tf_op jit(solution)/shard_map/td,kdh->kth/dot_general | solution.py:32
  132.0 1.1 fusion.74
  133.2 0.5 all-gather.14.cloned.1.call-update
  133.7 0.2 all-gather.12.cloned.1.call-start
  133.9 0.4 all-gather.12.cloned.1.call-update
  135.0 50.7 %all-gather.16.cloned.1.call-done = bf16[1,3072,384]{1,2,0:T(8,128)(2,1)} async-done(((bf16[1,768,384]{1,2,0:T(8,128)(2,1)}), bf16[1,3072,384]{1,2,0:T(8,128)(2,1)}) %all-gather.16.cloned.1.call-update) | async-done | bytes 2359312 | tf_op jit(solution)/shard_map/all_gather | solution.py:40
  185.6 16.2 %fusion.75 = (f32[3,768]{1,0:T(4,128)S(1)}, f32[3,768,3072]{2,1,0:T(8,128)}) fusion(pred[3072]{0:T(1024)(128)(4,1)S(1)} %fusion.68, bf16[768,3,128]{0,2,1:T(8,128)(2,1)S(1)} %bitcast.89, bf16[3072,3,128]{0,2,1:T(8,128)(2,1)} %bitcast.90), kind=kOutput, calls=%fused_computation.79 | convolution fusion | flops 1847331840 | bytes 31272960 | tf_op jit(solution)/shard_map/sub | solution.py:63
  201.9 44.3 %all-gather.14.cloned.1.call-done = bf16[1,3072,384]{1,2,0:T(8,128)(2,1)} async-done(((bf16[1,768,384]{1,2,0:T(8,128)(2,1)}), bf16[1,3072,384]{1,2,0:T(8,128)(2,1)}) %all-gather.14.cloned.1.call-update) | async-done | bytes 2359312 | tf_op jit(solution)/shard_map/all_gather | solution.py:41
  246.2 12.1 %fusion.45 = bf16[768,3,128]{0,2,1:T(8,128)(2,1)S(1)} fusion(bf16[3072,3,128]{0,2,1:T(8,128)(2,1)} %bitcast.91, f32[3,768,3072]{2,1,0:T(8,128)} %get-tuple-element.10, f32[3,768]{1,0:T(4,128)S(1)} %get-tuple-element.9), kind=kOutput, calls=%fused_computation.38 | convolution fusion | flops 1826390016 | bytes 31269888 | tf_op jit(solution)/shard_map/hqk,khd->qhd/dot_general | solution.py:65
  258.2 0.7 reshape.103
  258.9 1.4 copy.22
  260.3 3.5 all-to-all-start
  263.8 19.6 %all-gather.12.cloned.1.call-done = bf16[3072,384]{1,0:T(8,128)(2,1)} async-done(((bf16[192,384]{1,0:T(8,128)(2,1)}), bf16[3072,384]{1,0:T(8,128)(2,1)}) %all-gather.12.cloned.1.call-update) | async-done | bytes 2359312 | tf_op jit(solution)/shard_map/all_gather | solution.py:71
  283.5 6.3 stack.2
  289.8 5.9 all-to-all-start.1
  295.8 0.0 all-reduce.3.cloned.1.call-start
  297.3 107.0 %all_gather.23 = bf16[64,1536]{1,0:T(8,128)(2,1)S(1)} all-gather(bf16[64,384]{1,0:T(8,128)(2,1)S(1)} %copy-done.2), channel_id=1, replica_groups=mesh['fsdp'=16,'uly'=4,'blk'=4] {'uly'}, dimensions={1}, use_global_device_ids=true | all-gather | bytes 245760 | tf_op jit(solution)/shard_map/all_gather | solution.py:78
  404.3 0.1 copy.23
  404.3 0.3 convolution_convert_fusion.1
  404.6 2.8 fusion.38
  408.1 38.5 %psum.21 = f32[]{:T(128)} all-reduce(f32[]{:T(128)S(6)} %div.64), channel_id=1, replica_groups=mesh['fsdp'=16,'uly'=4,'blk'=4] {'uly','blk'}, use_global_device_ids=true, to_apply=%region_4.5 | all-reduce | flops 1 | bytes 8 | tf_op jit(solution)/shard_map/psum | solution.py:105
  447.4 1.3 fusion.73
  448.7 1.7 fusion.46
  450.4 8.8 %fusion.31 = bf16[1,192,3072]{2,1,0:T(8,128)(2,1)} fusion(bf16[4,3072,384]{2,1,0:T(8,128)(2,1)} %all-to-all-done.1, bf16[1,192,3072]{2,1,0:T(8,128)(2,1)} %param.10, bf16[1,192,3072]{2,1,0:T(8,128)(2,1)} %param.9, f32[]{:T(128)S(6)} %mul.121, f32[]{:T(128)S(6)} %mul.118, bf16[4,192,384]{2,1,0:T(8,128)(2,1)} %copy-done.1), kind=kOutput, calls=%fused_computation.25 | convolution fusion | flops 1818427392 | bytes 13565960 | tf_op jit(solution)/shard_map/dot_general | solution.py:80
  459.2 252.1 %all-reduce.3.cloned.1.call-done = (f32[64,1536]{1,0:T(8,128)}, f32[64,3072]{1,0:T(8,128)}) async-done(((f32[64,1536]{1,0:T(8,128)}, f32[64,3072]{1,0:T(8,128)}), (f32[64,1536]{1,0:T(8,128)}, f32[64,3072]{1,0:T(8,128)})) %all-reduce.3.cloned.1.call-update) | async-done | bytes 1179664 | tf_op jit(solution)/shard_map/psum | solution.py:124
  711.3 1.5 constant_dynamic-slice_fusion
  712.9 2.1 copy.29
  (18 shorter events, 0.3 us)
Async XLA Ops:
  7.2 397.5 %copy-start = (bf16[64,3072]{1,0:T(8,128)(2,1)S(1)}, bf16[64,3072]{1,0:T(8,128)(2,1)}, u32[]{:S(2)}) copy-start(bf16[64,3072]{1,0:T(8,128)(2,1)} %param.14) | copy-start | bytes 1179652
  7.2 63.2 %all-gather.8.cloned.1.call-start = ((), (), s32[]{:S(2)}) async-start(), calls=%async_computation.2 | async-start | bytes 5898240 | tf_op jit(solution)/shard_map/all_gather | solution.py:31
  11.5 110.2 %all-gather.10.cloned.1.call-start = ((), (), s32[]{:S(2)}) async-start(), calls=%async_computation.3 | async-start | bytes 7520256 | tf_op jit(solution)/shard_map/all_gather | solution.py:35
  12.2 173.4 %all-gather.16.cloned.1.call-start = ((), (), s32[]{:S(2)}) async-start(), calls=%async_computation.6 | async-start | bytes 2949120 | tf_op jit(solution)/shard_map/all_gather | solution.py:40
  133.1 113.0 %all-gather.14.cloned.1.call-start = ((), (), s32[]{:S(2)}) async-start(), calls=%async_computation.5 | async-start | bytes 2949120 | tf_op jit(solution)/shard_map/all_gather | solution.py:41
  133.7 149.7 %all-gather.12.cloned.1.call-start = ((), (), s32[]{:S(2)}) async-start(), calls=%async_computation.4 | async-start | bytes 2506752 | tf_op jit(solution)/shard_map/all_gather | solution.py:71
  260.3 23.1 %all-to-all-start = ((bf16[4,192,384]{2,1,0:T(8,128)(2,1)}), bf16[4,192,384]{2,1,0:T(8,128)(2,1)S(1)}, u32[]{:S(2)}, u32[]{:S(2)}) async-start(bf16[4,192,384]{2,1,0:T(8,128)(2,1)} %copy.22), calls=%async_computation | async-start | bytes 1179648 | tf_op jit(solution)/shard_map/all_to_all | solution.py:73
  283.5 120.8 %copy-start.1 = (bf16[4,192,384]{2,1,0:T(8,128)(2,1)}, bf16[4,192,384]{2,1,0:T(8,128)(2,1)S(1)}, u32[]{:S(2)}) copy-start(bf16[4,192,384]{2,1,0:T(8,128)(2,1)S(1)} %all-to-all-done) | copy-start | bytes 1769476
  289.8 7.4 %copy-start.2 = (bf16[64,384]{1,0:T(8,128)(2,1)S(1)}, bf16[64,384]{1,0:T(8,128)(2,1)}, u32[]{:S(2)}) copy-start(bf16[64,384]{1,0:T(8,128)(2,1)} %param.13) | copy-start | bytes 147460
  289.8 160.6 %all-to-all-start.1 = ((bf16[4,3072,384]{2,1,0:T(8,128)(2,1)}), bf16[4,3072,384]{2,1,0:T(8,128)(2,1)}, u32[]{:S(2)}, u32[]{:S(2)}) async-start(bf16[4,3072,384]{2,1,0:T(8,128)(2,1)} %stack.2), calls=%async_computation.1 | async-start | bytes 18874368 | tf_op jit(solution)/shard_map/all_to_all | solution.py:76
  295.8 415.6 %all-reduce.3.cloned.1.call-start = ((), (), s32[]{:S(2)}) async-start(), calls=%async_computation.7 | async-start | bytes 2359296 | tf_op jit(solution)/shard_map/psum | solution.py:124
Sparse Core Ops, SparseCore 0:
  11.6 58.6 all-gather.7
  72.1 49.4 all-gather.9
  133.3 52.3 all-gather.15
  187.9 58.2 all-gather.13
  247.8 35.5 all-gather.11
  450.5 260.7 all-reduce.2
